TPU v7x, 32 devices: a whole 2x2x4 slice. The times are simulated.
32 devices in a mesh: groups: 2 (over y), ctx: 4 (over z), mp: 4 (over x, core).
Axes of the slice: x: 2, y: 2, z: 4, core: 2. Of those that a mesh axis runs over, the one named last changes fastest.
Arguments:
- queries: bfloat16 [2048, 4096], P(('groups', 'ctx'), 'mp'), parts along dimension 0, may hold values from -18 to 18
- keyvals: bfloat16 [2048, 512], P(('groups', 'ctx', 'mp')), parts along dimension 0, may hold values from -6 to 6
- segment_ids: int32 [2048], P('groups'), parts along dimension 0, may hold values from 0 to 2, never falling along the last dimension, each value on 1 to 512 neighbouring positions
- residual: bfloat16 [2048, 4096], P(('groups', 'ctx', 'mp')), parts along dimension 0, may hold values from -180 to 180
- out_weight: bfloat16 [4096, 4096], P('mp', 'ctx'), may hold values from -0.375 to 0.375
- lru_weight: bfloat16 [4096, 4096], P('ctx', 'mp'), may hold values from -0.09375 to 0.09375
- conv_weight: float32 [4, 4096], P(None, 'mp'), may hold values from -3 to 3
- gate_decay_w: bfloat16 [16, 256, 256], P('mp'), may hold values from -0.375 to 0.375
- gate_input_w: bfloat16 [16, 256, 256], P('mp'), may hold values from -0.375 to 0.375
- gate_decay_b: float32 [4096], P('mp'), may hold values from -3 to 3
- gate_input_b: float32 [4096], P('mp'), may hold values from -3 to 3
- decay_codes: int32 [4096], P('mp'), may hold values from 0 to 15
- norm_gain: float32 [4096], replicated, may hold values from 0.1 to 1.9
Outputs:
- resid_out: bfloat16 [2048, 4096], P(('groups', 'ctx', 'mp')), parts along dimension 0
- lru_out: bfloat16 [2048, 4096], P(('groups', 'ctx'), 'mp'), parts along dimension 0
There are 2 independent parts, one for each index of `groups`. A program takes and returns all parts, laid end to end along the dimension named above; an argument that names none is the same for every part. Nothing has to cross between parts.
All inputs are finite; a program needn't handle non-finite values.
Results may differ from a plain program's by a relative error of at most 0.017.
Values may be sent and summed in bfloat16 or wider, within the bound.
No kernel may reach another device: no remote copies, remote signals or barrier semaphores. Data moves between devices by JAX's collectives and lax.ppermute only.
A program may use at most 64 MiB of HBM per device.

v0:
```python
import math
import jax
import jax.numpy as jnp
from jax import lax
from jax.sharding import PartitionSpec as P

HD = 256
WIN = 2048
CONV = 4
LEVELS = 16
BW = 256


def shifted_2(value, axis, steps):
    count = lax.axis_size(axis)
    initial, last = (max(0, -steps), min(count, count - steps))
    return lax.ppermute(value, axis, [(source, source + steps) for source in range(initial, last)])


def decay_rates():
    levels = jnp.arange(LEVELS, dtype=jnp.float32)
    return 0.006 * jnp.exp(-levels * (math.log(3000.0) / (LEVELS - 1)))


def chain_link(former, latter):
    return (former[0] * latter[0], latter[0] * former[1] + latter[1])


def rms_scaled(values, norm_gain):
    value_f32 = values.astype(jnp.float32)
    inverse = lax.rsqrt(jnp.mean(value_f32 * value_f32, axis=-1, keepdims=True) + 1e-06)
    return (value_f32 * inverse * norm_gain).astype(jnp.bfloat16)


def attend_local(queries, keys_all, allowed):
    rows_here = queries.shape[0]
    heads_here = queries.shape[1] // HD
    query_heads = queries.reshape(rows_here, heads_here, HD)
    score_scale = 1.0 / math.sqrt(HD)
    scores = (
        jnp.einsum("thd,kd->htk", query_heads, keys_all[:, :HD], preferred_element_type=jnp.float32)
        * score_scale
    )
    scores = jnp.where(allowed[None], scores, -1e30)
    row_top = jnp.max(scores, axis=-1, keepdims=True)
    weights = jnp.exp(scores - row_top)
    probs = (weights / jnp.sum(weights, axis=-1, keepdims=True)).astype(jnp.bfloat16)
    gathered = jnp.einsum(
        "htk,kd->thd", probs, keys_all[:, HD:], preferred_element_type=jnp.float32
    )
    return gathered.reshape(rows_here, heads_here * HD).astype(jnp.bfloat16)


def local(
    queries,
    keyvals,
    segment_ids,
    residual,
    out_weight,
    lru_weight,
    conv_weight,
    gate_decay_w,
    gate_input_w,
    gate_decay_b,
    gate_input_b,
    decay_codes,
    norm_gain,
):
    rows_here = queries.shape[0]
    ctx_index = lax.axis_index("ctx")
    back_blocks = WIN // rows_here
    own_kv = lax.all_gather(keyvals, "mp", axis=0, tiled=True)
    earlier = []
    moving = own_kv
    for offset in range(back_blocks):
        moving = shifted_2(moving, "ctx", 1)
        earlier = [moving] + earlier
    keys_all = jnp.concatenate(earlier + [own_kv], axis=0)
    pad_seg = jnp.concatenate([jnp.full((WIN,), -1, jnp.int32), segment_ids])
    query_seg = lax.dynamic_slice_in_dim(segment_ids, ctx_index * rows_here, rows_here)
    key_seg = lax.dynamic_slice_in_dim(
        pad_seg, ctx_index * rows_here, (back_blocks + 1) * rows_here
    )
    query_pos = ctx_index * rows_here + jnp.arange(rows_here, dtype=jnp.int32)
    key_pos = (ctx_index - back_blocks) * rows_here + jnp.arange(
        (back_blocks + 1) * rows_here, dtype=jnp.int32
    )
    distance = query_pos[:, None] - key_pos[None, :]
    allowed = (distance >= 0) & (distance < WIN) & (query_seg[:, None] == key_seg[None, :])
    attended = attend_local(queries, keys_all, allowed)
    head_part = jnp.dot(
        attended,
        lax.all_gather(out_weight, "ctx", axis=1, tiled=True),
        preferred_element_type=jnp.float32,
    )
    summed = lax.psum_scatter(
        head_part.astype(jnp.bfloat16), "mp", scatter_dimension=0, tiled=True
    ).astype(jnp.float32)
    resid_out = (summed + residual.astype(jnp.float32)).astype(jnp.bfloat16)
    normed = lax.all_gather(rms_scaled(resid_out, norm_gain), "mp", axis=0, tiled=True)
    channels = lru_weight.shape[1]
    lru_in = jnp.dot(
        normed,
        lax.all_gather(lru_weight, "ctx", axis=0, tiled=True),
        preferred_element_type=jnp.float32,
    ).astype(jnp.bfloat16)
    rim_rows = shifted_2(lru_in[rows_here - (CONV - 1) :], "ctx", 1)
    extended = jnp.concatenate([rim_rows, lru_in], axis=0)
    ext_seg = lax.dynamic_slice_in_dim(
        pad_seg, ctx_index * rows_here + WIN - (CONV - 1), rows_here + CONV - 1
    )
    conv_acc = jnp.zeros((rows_here, channels), jnp.float32)
    for offset in range(CONV):
        lag_rows = CONV - 1 - offset
        shifted = extended[lag_rows : lag_rows + rows_here].astype(jnp.float32)
        same_doc = (ext_seg[lag_rows : lag_rows + rows_here] == query_seg)[:, None]
        conv_acc = conv_acc + jnp.where(same_doc, conv_weight[offset] * shifted, 0.0)
    conv_out = conv_acc.astype(jnp.bfloat16)
    blocks_here = channels // BW
    grouped = conv_out.reshape(rows_here, blocks_here, BW)
    decay_gate = jax.nn.sigmoid(
        jnp.einsum(
            "tbi,bij->tbj", grouped, gate_decay_w, preferred_element_type=jnp.float32
        ).reshape(rows_here, channels)
        + gate_decay_b
    )
    input_gate = jax.nn.sigmoid(
        jnp.einsum(
            "tbi,bij->tbj", grouped, gate_input_w, preferred_element_type=jnp.float32
        ).reshape(rows_here, channels)
        + gate_input_b
    )
    levels = jnp.arange(LEVELS, dtype=jnp.int32)
    decay_rate = jnp.sum(
        jnp.where(decay_codes[:, None] == levels[None, :], decay_rates()[None, :], 0.0), axis=1
    )
    log_decay = -8.0 * decay_gate * decay_rate
    restart = (query_seg != ext_seg[CONV - 2 : CONV - 2 + rows_here])[:, None]
    keep_factor = jnp.where(restart, 0.0, jnp.exp(log_decay))
    input_scale = jnp.where(restart, 1.0, jnp.sqrt(-jnp.expm1(2.0 * log_decay)))
    driven = input_scale * input_gate * conv_out.astype(jnp.float32)
    cum_keep, local_state = lax.associative_scan(chain_link, (keep_factor, driven), axis=0)
    block_keep = cum_keep[rows_here - 1]
    block_state = local_state[rows_here - 1]

    def relay_turn(turn_index, state_in):
        return shifted_2(block_keep * state_in + block_state, "ctx", 1)

    incoming = lax.fori_loop(0, lax.axis_size("ctx") - 1, relay_turn, jnp.zeros_like(block_state))
    states = local_state + cum_keep * incoming[None, :]
    return (resid_out, states.astype(jnp.bfloat16))


def solution(mesh):
    in_specs = (
        P(("groups", "ctx"), "mp"),
        P(("groups", "ctx", "mp"), None),
        P("groups"),
        P(("groups", "ctx", "mp"), None),
        P("mp", "ctx"),
        P("ctx", "mp"),
        P(None, "mp"),
        P("mp", None, None),
        P("mp", None, None),
        P("mp"),
        P("mp"),
        P("mp"),
        P(),
    )
    out_specs = (P(("groups", "ctx", "mp"), None), P(("groups", "ctx"), "mp"))
    return jax.shard_map(local, mesh=mesh, in_specs=in_specs, out_specs=out_specs, check_vma=False)
```

profile of v0, /device:TPU:0, one launch (start us, length us, event | category | flops | bytes accessed | tf_op | source)
XLA Modules:
  0.0 554.3 jit_solution(5232723126797398906)
XLA Ops:
  8.0 7.4 %all_gather.12 = bf16[256,512]{1,0:T(8,128)(2,1)S(1)} all-gather(bf16[64,512]{1,0:T(8,128)(2,1)} %param.16), channel_id=1, replica_groups=mesh['groups'=2,'ctx'=4,'mp'=4] {'mp'}, dimensions={0}, use_global_device_ids=true | all-gather | bytes 327680 | tf_op jit(solution)/shard_map/all_gather | solution.py:72
  18.9 9.3 %collective-permute-done.1 = bf16[256,512]{1,0:T(8,128)(2,1)S(1)} collective-permute-done((bf16[256,512]{1,0:T(8,128)(2,1)S(1)}, bf16[256,512]{1,0:T(8,128)(2,1)S(1)}, u32[]{:S(2)}, u32[]{:S(2)}) %collective-permute-start.1) | collective-permute-done | bytes 262176 | tf_op jit(solution)/shard_map/ppermute | solution.py:17
  28.3 8.5 %collective-permute-start.2 = (bf16[256,512]{1,0:T(8,128)(2,1)S(1)}, bf16[256,512]{1,0:T(8,128)(2,1)S(1)}, u32[]{:S(2)}, u32[]{:S(2)}) collective-permute-start(bf16[256,512]{1,0:T(8,128)(2,1)S(1)} %collective-permute-done.1), channel_id=1, source_target_pairs={{0,4},{4,8},{8,12},{1,5},{5,9},{9,13},{2,6},{6,10},{10,14},{3,7},{... | collective-permute-start | bytes 786440 | tf_op jit(solution)/shard_map/ppermute | solution.py:17
  36.8 11.2 %collective-permute-done.2 = bf16[256,512]{1,0:T(8,128)(2,1)S(1)} collective-permute-done((bf16[256,512]{1,0:T(8,128)(2,1)S(1)}, bf16[256,512]{1,0:T(8,128)(2,1)S(1)}, u32[]{:S(2)}, u32[]{:S(2)}) %collective-permute-start.2) | collective-permute-done | bytes 262176 | tf_op jit(solution)/shard_map/ppermute | solution.py:17
  48.0 13.6 %collective-permute-start.3 = (bf16[256,512]{1,0:T(8,128)(2,1)S(1)}, bf16[256,512]{1,0:T(8,128)(2,1)S(1)}, u32[]{:S(2)}, u32[]{:S(2)}) collective-permute-start(bf16[256,512]{1,0:T(8,128)(2,1)S(1)} %collective-permute-done.2), channel_id=1, source_target_pairs={{0,4},{4,8},{8,12},{1,5},{5,9},{9,13},{2,6},{6,10},{10,14},{3,7},{... | collective-permute-start | bytes 786440 | tf_op jit(solution)/shard_map/ppermute | solution.py:17
  61.6 10.2 %collective-permute-done.3 = bf16[256,512]{1,0:T(8,128)(2,1)S(1)} collective-permute-done((bf16[256,512]{1,0:T(8,128)(2,1)S(1)}, bf16[256,512]{1,0:T(8,128)(2,1)S(1)}, u32[]{:S(2)}, u32[]{:S(2)}) %collective-permute-start.3) | collective-permute-done | bytes 262176 | tf_op jit(solution)/shard_map/ppermute | solution.py:17
  71.8 12.3 %collective-permute-start.4 = (bf16[256,512]{1,0:T(8,128)(2,1)S(1)}, bf16[256,512]{1,0:T(8,128)(2,1)S(1)}, u32[]{:S(2)}, u32[]{:S(2)}) collective-permute-start(bf16[256,512]{1,0:T(8,128)(2,1)S(1)} %collective-permute-done.3), channel_id=1, source_target_pairs={{0,4},{4,8},{8,12},{1,5},{5,9},{9,13},{2,6},{6,10},{10,14},{3,7},{... | collective-permute-start | bytes 786440 | tf_op jit(solution)/shard_map/ppermute | solution.py:17
  84.1 9.6 %collective-permute-done.4 = bf16[256,512]{1,0:T(8,128)(2,1)S(1)} collective-permute-done((bf16[256,512]{1,0:T(8,128)(2,1)S(1)}, bf16[256,512]{1,0:T(8,128)(2,1)S(1)}, u32[]{:S(2)}, u32[]{:S(2)}) %collective-permute-start.4) | collective-permute-done | bytes 262176 | tf_op jit(solution)/shard_map/ppermute | solution.py:17
  93.7 11.3 %collective-permute-start.5 = (bf16[256,512]{1,0:T(8,128)(2,1)S(1)}, bf16[256,512]{1,0:T(8,128)(2,1)S(1)}, u32[]{:S(2)}, u32[]{:S(2)}) collective-permute-start(bf16[256,512]{1,0:T(8,128)(2,1)S(1)} %collective-permute-done.4), channel_id=1, source_target_pairs={{0,4},{4,8},{8,12},{1,5},{5,9},{9,13},{2,6},{6,10},{10,14},{3,7},{... | collective-permute-start | bytes 786440 | tf_op jit(solution)/shard_map/ppermute | solution.py:17
  105.0 9.7 %collective-permute-done.5 = bf16[256,512]{1,0:T(8,128)(2,1)S(1)} collective-permute-done((bf16[256,512]{1,0:T(8,128)(2,1)S(1)}, bf16[256,512]{1,0:T(8,128)(2,1)S(1)}, u32[]{:S(2)}, u32[]{:S(2)}) %collective-permute-start.5) | collective-permute-done | bytes 262176 | tf_op jit(solution)/shard_map/ppermute | solution.py:17
  114.6 13.8 %collective-permute-start.6 = (bf16[256,512]{1,0:T(8,128)(2,1)S(1)}, bf16[256,512]{1,0:T(8,128)(2,1)S(1)}, u32[]{:S(2)}, u32[]{:S(2)}) collective-permute-start(bf16[256,512]{1,0:T(8,128)(2,1)S(1)} %collective-permute-done.5), channel_id=1, source_target_pairs={{0,4},{4,8},{8,12},{1,5},{5,9},{9,13},{2,6},{6,10},{10,14},{3,7},{... | collective-permute-start | bytes 786440 | tf_op jit(solution)/shard_map/ppermute | solution.py:17
  128.7 9.4 %collective-permute-done.6 = bf16[256,512]{1,0:T(8,128)(2,1)S(1)} collective-permute-done((bf16[256,512]{1,0:T(8,128)(2,1)S(1)}, bf16[256,512]{1,0:T(8,128)(2,1)S(1)}, u32[]{:S(2)}, u32[]{:S(2)}) %collective-permute-start.6) | collective-permute-done | bytes 262176 | tf_op jit(solution)/shard_map/ppermute | solution.py:17
  138.1 9.9 %collective-permute-start.7 = (bf16[256,512]{1,0:T(8,128)(2,1)S(1)}, bf16[256,512]{1,0:T(8,128)(2,1)S(1)}, u32[]{:S(2)}, u32[]{:S(2)}) collective-permute-start(bf16[256,512]{1,0:T(8,128)(2,1)S(1)} %collective-permute-done.6), channel_id=1, source_target_pairs={{0,4},{4,8},{8,12},{1,5},{5,9},{9,13},{2,6},{6,10},{10,14},{3,7},{... | collective-permute-start | bytes 786440 | tf_op jit(solution)/shard_map/ppermute | solution.py:17
  148.1 9.5 %collective-permute-done.7 = bf16[256,512]{1,0:T(8,128)(2,1)S(1)} collective-permute-done((bf16[256,512]{1,0:T(8,128)(2,1)S(1)}, bf16[256,512]{1,0:T(8,128)(2,1)S(1)}, u32[]{:S(2)}, u32[]{:S(2)}) %collective-permute-start.7) | collective-permute-done | bytes 262176 | tf_op jit(solution)/shard_map/ppermute | solution.py:17
  157.6 13.0 %collective-permute-start.8 = (bf16[256,512]{1,0:T(8,128)(2,1)S(1)}, bf16[256,512]{1,0:T(8,128)(2,1)S(1)}, u32[]{:S(2)}, u32[]{:S(2)}) collective-permute-start(bf16[256,512]{1,0:T(8,128)(2,1)S(1)} %collective-permute-done.7), channel_id=1, source_target_pairs={{0,4},{4,8},{8,12},{1,5},{5,9},{9,13},{2,6},{6,10},{10,14},{3,7},{... | collective-permute-start | bytes 786440 | tf_op jit(solution)/shard_map/ppermute | solution.py:17
  172.2 8.0 %collective-permute-done.8 = bf16[256,512]{1,0:T(8,128)(2,1)S(1)} collective-permute-done((bf16[256,512]{1,0:T(8,128)(2,1)S(1)}, bf16[256,512]{1,0:T(8,128)(2,1)S(1)}, u32[]{:S(2)}, u32[]{:S(2)}) %collective-permute-start.8) | collective-permute-done | bytes 262176 | tf_op jit(solution)/shard_map/ppermute | solution.py:17
  186.5 6.0 %fusion.8 = bf16[256,4,256]{2,0,1:T(8,128)(2,1)S(1)} fusion(f32[4,256]{1,0:T(4,128)S(1)} %fusion.53, bf16[2304,512]{1,0:T(8,128)(2,1)} %copy-done.12, pred[256,2304]{0,1:T(8,128)(4,1)S(1)} %fusion.7, bf16[32,4,8,256]{3,2,1,0:T(8,128)(2,1)S(1)} %bitcast.79), kind=kOutput, calls=%fused_computation.17 | convolution fusion | flops 2427981056 | bytes 4001792 | tf_op jit(solution)/shard_map/htk,kd->thd/dot_general | solution.py:48
  192.5 6.9 %all-gather.4.cloned.1.call-done = bf16[1024,4096]{1,0:T(8,128)(2,1)} async-done(((bf16[1024,1024]{1,0:T(8,128)(2,1)}), bf16[1024,4096]{1,0:T(8,128)(2,1)}) %all-gather.4.cloned.1.call-update) | async-done | bytes 8388624 | tf_op jit(solution)/shard_map/all_gather | solution.py:93
  199.5 7.1 %convolution_convert_fusion = bf16[256,4096]{1,0:T(8,128)(2,1)} fusion(bf16[256,1024]{0,1:T(8,128)(2,1)S(1)} %bitcast.71, bf16[1024,4096]{1,0:T(8,128)(2,1)} %all-gather.4.cloned.1.call-done), kind=kOutput, calls=%fused_computation.6 | convolution fusion | flops 2148532224 | bytes 11010048 | tf_op jit(solution)/shard_map/dot_general | solution.py:91
  207.6 33.9 %reduce-scatter.2.cloned.1.call-done = bf16[64,4096]{1,0:T(8,128)(2,1)} async-done(((bf16[256,4096]{1,0:T(8,128)(2,1)}), bf16[64,4096]{1,0:T(8,128)(2,1)}) %reduce-scatter.2.cloned.1.call-update) | async-done | bytes 524304 | tf_op jit(solution)/shard_map/reduce_scatter | solution.py:96
  244.8 147.9 %all-gather.8.cloned.1.call-done = bf16[4096,1024]{1,0:T(8,128)(2,1)} async-done(((bf16[1024,1024]{1,0:T(8,128)(2,1)}), bf16[4096,1024]{1,0:T(8,128)(2,1)}) %all-gather.8.cloned.1.call-update) | async-done | bytes 8388624 | tf_op jit(solution)/shard_map/all_gather | solution.py:104
  392.8 22.8 %all-gather.6.cloned.1.call-done = bf16[256,4096]{1,0:T(8,128)(2,1)} async-done(((bf16[64,4096]{1,0:T(8,128)(2,1)}), bf16[256,4096]{1,0:T(8,128)(2,1)}) %all-gather.6.cloned.1.call-update) | async-done | bytes 2097168 | tf_op jit(solution)/shard_map/all_gather | solution.py:100
  415.5 6.3 %convolution_convert_fusion.1 = bf16[256,1024]{1,0:T(8,128)(2,1)S(1)} fusion(bf16[256,4096]{1,0:T(8,128)(2,1)} %all-gather.6.cloned.1.call-done, bf16[4096,1024]{1,0:T(8,128)(2,1)} %all-gather.8.cloned.1.call-done), kind=kOutput, calls=%fused_computation.18 | convolution fusion | flops 2147745792 | bytes 11010048 | tf_op jit(solution)/shard_map/dot_general | solution.py:102
  528.5 16.5 %while.10 = (s32[]{:T(128)}, f32[1024]{0:T(1024)S(1)}, f32[1024]{0:T(1024)S(1)}, f32[1024]{0:T(1024)S(1)}, s32[]{:T(128)}) while((s32[]{:T(128)}, f32[1024]{0:T(1024)S(1)}, f32[1024]{0:T(1024)S(1)}, f32[1024]{0:T(1024)S(1)}, s32[]{:T(128)}) %tuple.63), condition=%wide.region_6.7_spmd, body=%wide.region_5.6_spmd.sunk | while | flops 2050 | bytes 32869 | solution.py:149
  (235 shorter events, 141.8 us)
Async XLA Ops:
  7.2 420.2 %copy-start = (bf16[4,256,256]{2,1,0:T(8,128)(2,1)S(1)}, bf16[4,256,256]{2,1,0:T(8,128)(2,1)}, u32[]{:S(2)}) copy-start(bf16[4,256,256]{2,1,0:T(8,128)(2,1)} %param.22) | copy-start | bytes 1572868
  7.2 121.3 %copy-start.13 = (s32[1024]{0:T(1024)S(1)}, s32[1024]{0:T(1024)}, u32[]{:S(2)}) copy-start(s32[1024]{0:T(1024)} %param.17) | copy-start | bytes 12292
  7.2 192.3 %all-gather.4.cloned.1.call-start = ((), (), s32[]{:S(2)}) async-start(), calls=%async_computation.1 | async-start | bytes 10485760 | tf_op jit(solution)/shard_map/all_gather | solution.py:93
  7.9 233.6 %reduce-scatter.2.cloned.1.call-start = ((), (), s32[]{:S(2)}) async-start(), calls=%async_computation.2 | async-start | bytes 2621440 | tf_op jit(solution)/shard_map/reduce_scatter | solution.py:96
  15.4 12.9 %collective-permute-start.1 = (bf16[256,512]{1,0:T(8,128)(2,1)S(1)}, bf16[256,512]{1,0:T(8,128)(2,1)S(1)}, u32[]{:S(2)}, u32[]{:S(2)}) collective-permute-start(bf16[256,512]{1,0:T(8,128)(2,1)S(1)} %all_gather.12), channel_id=1, source_target_pairs={{0,4},{4,8},{8,12},{1,5},{5,9},{9,13},{2,6},{6,10},{10,14},{3,7},{... | collective-permute-start | bytes 786440 | tf_op jit(solution)/shard_map/ppermute | solution.py:17
  28.3 19.7 %collective-permute-start.2 = (bf16[256,512]{1,0:T(8,128)(2,1)S(1)}, bf16[256,512]{1,0:T(8,128)(2,1)S(1)}, u32[]{:S(2)}, u32[]{:S(2)}) collective-permute-start(bf16[256,512]{1,0:T(8,128)(2,1)S(1)} %collective-permute-done.1), channel_id=1, source_target_pairs={{0,4},{4,8},{8,12},{1,5},{5,9},{9,13},{2,6},{6,10},{10,14},{3,7},{... | collective-permute-start | bytes 786440 | tf_op jit(solution)/shard_map/ppermute | solution.py:17
  48.0 23.8 %collective-permute-start.3 = (bf16[256,512]{1,0:T(8,128)(2,1)S(1)}, bf16[256,512]{1,0:T(8,128)(2,1)S(1)}, u32[]{:S(2)}, u32[]{:S(2)}) collective-permute-start(bf16[256,512]{1,0:T(8,128)(2,1)S(1)} %collective-permute-done.2), channel_id=1, source_target_pairs={{0,4},{4,8},{8,12},{1,5},{5,9},{9,13},{2,6},{6,10},{10,14},{3,7},{... | collective-permute-start | bytes 786440 | tf_op jit(solution)/shard_map/ppermute | solution.py:17
  71.8 21.9 %collective-permute-start.4 = (bf16[256,512]{1,0:T(8,128)(2,1)S(1)}, bf16[256,512]{1,0:T(8,128)(2,1)S(1)}, u32[]{:S(2)}, u32[]{:S(2)}) collective-permute-start(bf16[256,512]{1,0:T(8,128)(2,1)S(1)} %collective-permute-done.3), channel_id=1, source_target_pairs={{0,4},{4,8},{8,12},{1,5},{5,9},{9,13},{2,6},{6,10},{10,14},{3,7},{... | collective-permute-start | bytes 786440 | tf_op jit(solution)/shard_map/ppermute | solution.py:17
  93.7 21.0 %collective-permute-start.5 = (bf16[256,512]{1,0:T(8,128)(2,1)S(1)}, bf16[256,512]{1,0:T(8,128)(2,1)S(1)}, u32[]{:S(2)}, u32[]{:S(2)}) collective-permute-start(bf16[256,512]{1,0:T(8,128)(2,1)S(1)} %collective-permute-done.4), channel_id=1, source_target_pairs={{0,4},{4,8},{8,12},{1,5},{5,9},{9,13},{2,6},{6,10},{10,14},{3,7},{... | collective-permute-start | bytes 786440 | tf_op jit(solution)/shard_map/ppermute | solution.py:17
  114.6 23.4 %collective-permute-start.6 = (bf16[256,512]{1,0:T(8,128)(2,1)S(1)}, bf16[256,512]{1,0:T(8,128)(2,1)S(1)}, u32[]{:S(2)}, u32[]{:S(2)}) collective-permute-start(bf16[256,512]{1,0:T(8,128)(2,1)S(1)} %collective-permute-done.5), channel_id=1, source_target_pairs={{0,4},{4,8},{8,12},{1,5},{5,9},{9,13},{2,6},{6,10},{10,14},{3,7},{... | collective-permute-start | bytes 786440 | tf_op jit(solution)/shard_map/ppermute | solution.py:17
  138.1 19.5 %collective-permute-start.7 = (bf16[256,512]{1,0:T(8,128)(2,1)S(1)}, bf16[256,512]{1,0:T(8,128)(2,1)S(1)}, u32[]{:S(2)}, u32[]{:S(2)}) collective-permute-start(bf16[256,512]{1,0:T(8,128)(2,1)S(1)} %collective-permute-done.6), channel_id=1, source_target_pairs={{0,4},{4,8},{8,12},{1,5},{5,9},{9,13},{2,6},{6,10},{10,14},{3,7},{... | collective-permute-start | bytes 786440 | tf_op jit(solution)/shard_map/ppermute | solution.py:17
  157.6 22.6 %collective-permute-start.8 = (bf16[256,512]{1,0:T(8,128)(2,1)S(1)}, bf16[256,512]{1,0:T(8,128)(2,1)S(1)}, u32[]{:S(2)}, u32[]{:S(2)}) collective-permute-start(bf16[256,512]{1,0:T(8,128)(2,1)S(1)} %collective-permute-done.7), channel_id=1, source_target_pairs={{0,4},{4,8},{8,12},{1,5},{5,9},{9,13},{2,6},{6,10},{10,14},{3,7},{... | collective-permute-start | bytes 786440 | tf_op jit(solution)/shard_map/ppermute | solution.py:17
  206.5 35.0 %copy-start.4 = (bf16[64,4096]{1,0:T(8,128)(2,1)S(1)}, bf16[64,4096]{1,0:T(8,128)(2,1)}, u32[]{:S(2)}) copy-start(bf16[64,4096]{1,0:T(8,128)(2,1)} %param.18) | copy-start | bytes 1572868
  206.6 37.1 %copy-start.14 = (f32[4096]{0:T(1024)S(1)}, f32[4096]{0:T(1024)}, u32[]{:S(2)}) copy-start(f32[4096]{0:T(1024)} %param.27) | copy-start | bytes 49156
  206.6 38.1 %copy-start.25 = (s32[1024]{0:T(1024)S(1)}, s32[1024]{0:T(1024)}, u32[]{:S(2)}) copy-start(s32[1024]{0:T(1024)} %param.26) | copy-start | bytes 12292
  206.6 38.2 %copy-start.24 = (f32[4,1024]{1,0:T(4,128)S(1)}, f32[4,1024]{1,0:T(4,128)}, u32[]{:S(2)}) copy-start(f32[4,1024]{1,0:T(4,128)} %param.21) | copy-start | bytes 49156
  206.6 186.1 %all-gather.8.cloned.1.call-start = ((), (), s32[]{:S(2)}) async-start(), calls=%async_computation.4 | async-start | bytes 10485760 | tf_op jit(solution)/shard_map/all_gather | solution.py:104
  207.3 208.2 %all-gather.6.cloned.1.call-start = ((), (), s32[]{:S(2)}) async-start(), calls=%async_computation.3 | async-start | bytes 2621440 | tf_op jit(solution)/shard_map/all_gather | solution.py:100
  421.9 4.7 collective-permute-start.9
  504.4 8.9 %copy-start.7 = (f32[15,1024]{1,0:T(8,128)S(1)}, f32[15,1024]{1,0:T(8,128)}, u32[]{:S(2)}) copy-start(f32[15,1024]{1,0:T(8,128)} %slice.312) | copy-start | bytes 184324
  504.4 8.9 %copy-start.8 = (f32[15,1024]{1,0:T(8,128)S(1)}, f32[15,1024]{1,0:T(8,128)}, u32[]{:S(2)}) copy-start(f32[15,1024]{1,0:T(8,128)} %slice.345) | copy-start | bytes 184324
  528.5 5.5 collective-permute-start
  534.0 5.5 collective-permute-start
  539.5 5.5 collective-permute-start
  (21 other events, 81.1 us)
Sparse Core Ops, SparseCore 0:
  9.6 189.8 all-gather.3
  206.7 34.7 reduce-scatter.1
  243.1 149.6 all-gather.7
  394.7 20.7 all-gather.5
where the time goes:
time: 557 us; the launch traced here: 554 us
  waiting for transfers between devices  295 us (53%)
  starting transfers between devices  102 us (18%)
  local copies, waits for them, and re-layouts  77.2 us (14%)
  other arithmetic  32.9 us (6%)
  matrix products  24.8 us (4%)
  between operations  14.7 us (3%)
  blocking collectives  7.43 us (1%)
    all_gather x1, waiting for transfers between devices, local(): lax.all_gather(lru_weight, 'ctx', axis=0, tiled=True)  148 us
    ppermute x12, starting transfers between devices, shifted_2(): lax.ppermute(value, axis, [(source, source + steps) for source in range(i...  102 us
    ppermute x12, waiting for transfers between devices, shifted_2(): lax.ppermute(value, axis, [(source, source + steps) for source in range(i...  82.1 us
    slice x52, local copies, waits for them, and re-layouts, local(): lax.associative_scan(chain_link, (keep_factor, driven), axis=0)  61 us
    reduce_scatter x1, waiting for transfers between devices, local(): lax.psum_scatter(head_part.astype(jnp.bfloat16), 'mp', scatter_dimension=...  33.9 us
    all_gather x1, waiting for transfers between devices, local(): lax.all_gather(rms_scaled(resid_out, norm_gain), 'mp', axis=0, tiled=True)  22.8 us
    add x13, other arithmetic, chain_link(): return (former[0] * latter[0], latter[0] * former[1] + latter[1])  13.8 us
  transfers between devices with their start and end apart: 16, of which 16 were waited for; matrix products, arithmetic and copies ran while one was open for 3% of the time, Pallas kernels for 0%

commit v1 on v0

--- a/solution.py
+++ b/solution.py
@@ -1,3 +1,4 @@
+import functools
 import math
 import jax
 import jax.numpy as jnp
@@ -9,6 +10,27 @@
 CONV = 4
 LEVELS = 16
 BW = 256
+
+
+def _note_windows(shard_in, pos_dim):
+    k_now = list(shard_in.shape[1:])
+    k_now[pos_dim] *= shard_in.shape[0]
+    return jnp.moveaxis(shard_in, 0, pos_dim).reshape(k_now)
+
+
+def obtain_target_on_mesh(my_data, ax_name, row_dim):
+    nodes = lax.axis_size(ax_name)
+    pages = [(pp, (pp + 1) % nodes) for pp in range(nodes)]
+    in_order = [my_data]
+    while len(in_order) < nodes:
+        in_order.append(lax.ppermute(in_order[-1], ax_name, pages))
+    r_now = lax.axis_index(ax_name)
+    y = jnp.stack(in_order, axis=0)
+    in_order = y[(r_now - jnp.arange(nodes)) % nodes]
+    return _note_windows(in_order, row_dim)
+
+
+deliver_bars_on = functools.partial(obtain_target_on_mesh, ax_name="ctx", row_dim=0)
 
 
 def shifted_2(value, axis, steps):
@@ -100,9 +122,7 @@
     normed = lax.all_gather(rms_scaled(resid_out, norm_gain), "mp", axis=0, tiled=True)
     channels = lru_weight.shape[1]
     lru_in = jnp.dot(
-        normed,
-        lax.all_gather(lru_weight, "ctx", axis=0, tiled=True),
-        preferred_element_type=jnp.float32,
+        normed, deliver_bars_on(lru_weight), preferred_element_type=jnp.float32
     ).astype(jnp.bfloat16)
     rim_rows = shifted_2(lru_in[rows_here - (CONV - 1) :], "ctx", 1)
     extended = jnp.concatenate([rim_rows, lru_in], axis=0)

time: 557 us -> 530 us (0.952)
  waiting for transfers between devices: 295 us -> 247 us
  local copies, waits for them, and re-layouts: 77.2 us -> 93.1 us
  other arithmetic: 32.9 us -> 42.5 us
    all_gather x1 -> x0, waiting for transfers between devices: 148 us -> none  [local(): lax.all_gather(lru_weight, 'ctx', axis=0, tiled=True)]
    ppermute x0 -> x3, waiting for transfers between devices: none -> 92.2 us  [obtain_target_on_mesh(): in_order.append(lax.ppermute(in_order[-1], ax_name, pages))]
    ppermute x12, waiting for transfers between devices: 82.1 us -> 154 us  [shifted_2(): lax.ppermute(value, axis, [(source, source + steps) for source in range(i...]
    reduce_scatter x1, waiting for transfers between devices: 33.9 us -> 0.01 us  [local(): lax.psum_scatter(head_part.astype(jnp.bfloat16), 'mp', scatter_dimension=...]
    all_gather x1, waiting for transfers between devices: 22.8 us -> 0.01 us  [local(): lax.all_gather(rms_scaled(resid_out, norm_gain), 'mp', axis=0, tiled=True)]
    gather x0 -> x3, local copies, waits for them, and re-layouts: none -> 13.9 us  [obtain_target_on_mesh(): in_order = y[(r_now - jnp.arange(nodes)) % nodes]]
    ppermute x12, starting transfers between devices: 102 us -> 92.1 us  [shifted_2(): lax.ppermute(value, axis, [(source, source + steps) for source in range(i...]
    unnamed x0 -> x1, other arithmetic: none -> 7.75 us
  transfers between devices with their start and end apart: 16 -> 18, of which waited for: 16 -> 14; matrix products, arithmetic and copies ran while one was open for 3% -> 9% of each run, Pallas kernels for 0% -> 0%
where the time goes in v1:
time: 530 us; the launch traced here: 527 us
  waiting for transfers between devices  247 us (47%)
  starting transfers between devices  97.3 us (18%)
  local copies, waits for them, and re-layouts  93.1 us (18%)
  other arithmetic  42.5 us (8%)
  matrix products  25.1 us (5%)
  between operations  14.8 us (3%)
  blocking collectives  7.43 us (1%)
    ppermute x12, waiting for transfers between devices, shifted_2(): lax.ppermute(value, axis, [(source, source + steps) for source in range(i...  154 us
    ppermute x3, waiting for transfers between devices, obtain_target_on_mesh(): in_order.append(lax.ppermute(in_order[-1], ax_name, pages))  92.2 us
    ppermute x12, starting transfers between devices, shifted_2(): lax.ppermute(value, axis, [(source, source + steps) for source in range(i...  92.1 us
    slice x52, local copies, waits for them, and re-layouts, local(): lax.associative_scan(chain_link, (keep_factor, driven), axis=0)  61 us
    gather x3, local copies, waits for them, and re-layouts, obtain_target_on_mesh(): in_order = y[(r_now - jnp.arange(nodes)) % nodes]  13.9 us
    add x13, other arithmetic, chain_link(): return (former[0] * latter[0], latter[0] * former[1] + latter[1])  13.8 us
  transfers between devices with their start and end apart: 18, of which 14 were waited for; matrix products, arithmetic and copies ran while one was open for 9% of the time, Pallas kernels for 0%

profile of v1, /device:TPU:0, one launch (start us, length us, event | category | flops | bytes accessed | tf_op | source)
XLA Modules:
  0.0 527.0 jit_solution(13281096308157906650)
XLA Ops:
  8.0 7.4 %all_gather.9 = bf16[256,512]{1,0:T(8,128)(2,1)S(1)} all-gather(bf16[64,512]{1,0:T(8,128)(2,1)} %param.16), channel_id=1, replica_groups=mesh['groups'=2,'ctx'=4,'mp'=4] {'mp'}, dimensions={0}, use_global_device_ids=true | all-gather | bytes 327680 | tf_op jit(solution)/shard_map/all_gather | solution.py:94
  18.9 9.3 %collective-permute-done.1 = bf16[256,512]{1,0:T(8,128)(2,1)S(1)} collective-permute-done((bf16[256,512]{1,0:T(8,128)(2,1)S(1)}, bf16[256,512]{1,0:T(8,128)(2,1)S(1)}, u32[]{:S(2)}, u32[]{:S(2)}) %collective-permute-start.1) | collective-permute-done | bytes 262176 | tf_op jit(solution)/shard_map/ppermute | solution.py:39
  28.3 8.5 %collective-permute-start.2 = (bf16[256,512]{1,0:T(8,128)(2,1)S(1)}, bf16[256,512]{1,0:T(8,128)(2,1)S(1)}, u32[]{:S(2)}, u32[]{:S(2)}) collective-permute-start(bf16[256,512]{1,0:T(8,128)(2,1)S(1)} %collective-permute-done.1), channel_id=1, source_target_pairs={{0,4},{4,8},{8,12},{1,5},{5,9},{9,13},{2,6},{6,10},{10,14},{3,7},{... | collective-permute-start | bytes 786440 | tf_op jit(solution)/shard_map/ppermute | solution.py:39
  36.8 11.2 %collective-permute-done.2 = bf16[256,512]{1,0:T(8,128)(2,1)S(1)} collective-permute-done((bf16[256,512]{1,0:T(8,128)(2,1)S(1)}, bf16[256,512]{1,0:T(8,128)(2,1)S(1)}, u32[]{:S(2)}, u32[]{:S(2)}) %collective-permute-start.2) | collective-permute-done | bytes 262176 | tf_op jit(solution)/shard_map/ppermute | solution.py:39
  48.0 13.6 %collective-permute-start.3 = (bf16[256,512]{1,0:T(8,128)(2,1)S(1)}, bf16[256,512]{1,0:T(8,128)(2,1)S(1)}, u32[]{:S(2)}, u32[]{:S(2)}) collective-permute-start(bf16[256,512]{1,0:T(8,128)(2,1)S(1)} %collective-permute-done.2), channel_id=1, source_target_pairs={{0,4},{4,8},{8,12},{1,5},{5,9},{9,13},{2,6},{6,10},{10,14},{3,7},{... | collective-permute-start | bytes 786440 | tf_op jit(solution)/shard_map/ppermute | solution.py:39
  61.6 10.2 %collective-permute-done.3 = bf16[256,512]{1,0:T(8,128)(2,1)S(1)} collective-permute-done((bf16[256,512]{1,0:T(8,128)(2,1)S(1)}, bf16[256,512]{1,0:T(8,128)(2,1)S(1)}, u32[]{:S(2)}, u32[]{:S(2)}) %collective-permute-start.3) | collective-permute-done | bytes 262176 | tf_op jit(solution)/shard_map/ppermute | solution.py:39
  71.8 12.3 %collective-permute-start.4 = (bf16[256,512]{1,0:T(8,128)(2,1)S(1)}, bf16[256,512]{1,0:T(8,128)(2,1)S(1)}, u32[]{:S(2)}, u32[]{:S(2)}) collective-permute-start(bf16[256,512]{1,0:T(8,128)(2,1)S(1)} %collective-permute-done.3), channel_id=1, source_target_pairs={{0,4},{4,8},{8,12},{1,5},{5,9},{9,13},{2,6},{6,10},{10,14},{3,7},{... | collective-permute-start | bytes 786440 | tf_op jit(solution)/shard_map/ppermute | solution.py:39
  84.1 9.6 %collective-permute-done.4 = bf16[256,512]{1,0:T(8,128)(2,1)S(1)} collective-permute-done((bf16[256,512]{1,0:T(8,128)(2,1)S(1)}, bf16[256,512]{1,0:T(8,128)(2,1)S(1)}, u32[]{:S(2)}, u32[]{:S(2)}) %collective-permute-start.4) | collective-permute-done | bytes 262176 | tf_op jit(solution)/shard_map/ppermute | solution.py:39
  93.7 11.4 %collective-permute-start.5 = (bf16[256,512]{1,0:T(8,128)(2,1)S(1)}, bf16[256,512]{1,0:T(8,128)(2,1)S(1)}, u32[]{:S(2)}, u32[]{:S(2)}) collective-permute-start(bf16[256,512]{1,0:T(8,128)(2,1)S(1)} %collective-permute-done.4), channel_id=1, source_target_pairs={{0,4},{4,8},{8,12},{1,5},{5,9},{9,13},{2,6},{6,10},{10,14},{3,7},{... | collective-permute-start | bytes 786440 | tf_op jit(solution)/shard_map/ppermute | solution.py:39
  105.0 9.6 %collective-permute-done.5 = bf16[256,512]{1,0:T(8,128)(2,1)S(1)} collective-permute-done((bf16[256,512]{1,0:T(8,128)(2,1)S(1)}, bf16[256,512]{1,0:T(8,128)(2,1)S(1)}, u32[]{:S(2)}, u32[]{:S(2)}) %collective-permute-start.5) | collective-permute-done | bytes 262176 | tf_op jit(solution)/shard_map/ppermute | solution.py:39
  114.7 13.8 %collective-permute-start.6 = (bf16[256,512]{1,0:T(8,128)(2,1)S(1)}, bf16[256,512]{1,0:T(8,128)(2,1)S(1)}, u32[]{:S(2)}, u32[]{:S(2)}) collective-permute-start(bf16[256,512]{1,0:T(8,128)(2,1)S(1)} %collective-permute-done.5), channel_id=1, source_target_pairs={{0,4},{4,8},{8,12},{1,5},{5,9},{9,13},{2,6},{6,10},{10,14},{3,7},{... | collective-permute-start | bytes 786440 | tf_op jit(solution)/shard_map/ppermute | solution.py:39
  131.3 9.6 %collective-permute-done.6 = bf16[256,512]{1,0:T(8,128)(2,1)S(1)} collective-permute-done((bf16[256,512]{1,0:T(8,128)(2,1)S(1)}, bf16[256,512]{1,0:T(8,128)(2,1)S(1)}, u32[]{:S(2)}, u32[]{:S(2)}) %collective-permute-start.6) | collective-permute-done | bytes 262176 | tf_op jit(solution)/shard_map/ppermute | solution.py:39
  140.8 10.7 %collective-permute-start.7 = (bf16[256,512]{1,0:T(8,128)(2,1)S(1)}, bf16[256,512]{1,0:T(8,128)(2,1)}, u32[]{:S(2)}, u32[]{:S(2)}) collective-permute-start(bf16[256,512]{1,0:T(8,128)(2,1)S(1)} %collective-permute-done.6), channel_id=1, source_target_pairs={{0,4},{4,8},{8,12},{1,5},{5,9},{9,13},{2,6},{6,10},{10,14},{3,7},{... | collective-permute-start | bytes 786440 | tf_op jit(solution)/shard_map/ppermute | solution.py:39
  151.6 86.4 %collective-permute-done.7 = bf16[256,512]{1,0:T(8,128)(2,1)} collective-permute-done((bf16[256,512]{1,0:T(8,128)(2,1)S(1)}, bf16[256,512]{1,0:T(8,128)(2,1)}, u32[]{:S(2)}, u32[]{:S(2)}) %collective-permute-start.7) | collective-permute-done | bytes 262176 | tf_op jit(solution)/shard_map/ppermute | solution.py:39
  250.3 4.7 fusion.56
  254.9 6.3 %fusion.8 = bf16[256,4,256]{2,0,1:T(8,128)(2,1)S(1)} fusion(f32[4,256]{1,0:T(4,128)S(1)} %fusion.56, bf16[2304,512]{1,0:T(8,128)(2,1)} %copy-done.25, pred[256,2304]{0,1:T(8,128)(4,1)} %copy-done.5, bf16[32,4,8,256]{3,2,1,0:T(8,128)(2,1)} %bitcast.88), kind=kOutput, calls=%fused_computation.21 | convolution fusion | flops 2427981056 | bytes 4001792 | tf_op jit(solution)/shard_map/htk,kd->thd/dot_general | solution.py:70
  261.3 7.1 %convolution_convert_fusion = bf16[256,4096]{1,0:T(8,128)(2,1)} fusion(bf16[256,1024]{0,1:T(8,128)(2,1)S(1)} %bitcast.80, bf16[1024,4096]{1,0:T(8,128)(2,1)} %all-gather.3.cloned.1.call-done), kind=kOutput, calls=%fused_computation.10 | convolution fusion | flops 2148532224 | bytes 11010048 | tf_op jit(solution)/shard_map/dot_general | solution.py:113
  271.1 48.1 %collective-permute-done.10 = bf16[1024,1024]{1,0:T(8,128)(2,1)} collective-permute-done((bf16[1024,1024]{1,0:T(8,128)(2,1)}, bf16[1024,1024]{1,0:T(8,128)(2,1)}, u32[]{:S(2)}, u32[]{:S(2)}) %collective-permute-start.10) | collective-permute-done | bytes 2097184 | tf_op jit(solution)/shard_map/ppermute | solution.py:26
  322.5 44.1 %collective-permute-done.11 = bf16[1024,1024]{1,0:T(8,128)(2,1)} collective-permute-done((bf16[1024,1024]{1,0:T(8,128)(2,1)}, bf16[1024,1024]{1,0:T(8,128)(2,1)}, u32[]{:S(2)}, u32[]{:S(2)}) %collective-permute-start.11) | collective-permute-done | bytes 2097184 | tf_op jit(solution)/shard_map/ppermute | solution.py:26
  374.4 5.1 gather_fusion
  379.4 4.9 gather_fusion.1
  384.4 7.8 %pad_maximum_fusion.1 = bf16[4,1024,1024]{2,1,0:T(8,128)(2,1)} fusion(bf16[4,512,1024]{2,1,0:T(8,128)(2,1)} %gather_fusion.1, bf16[4,512,1024]{2,1,0:T(8,128)(2,1)} %gather_fusion), kind=kLoop, calls=%fused_computation.8 | loop fusion | flops 16777216 | bytes 16777216
  392.1 6.3 %convolution_convert_fusion.1 = bf16[256,1024]{1,0:T(8,128)(2,1)S(1)} fusion(bf16[256,4096]{1,0:T(8,128)(2,1)} %all-gather.5.cloned.1.call-done, bf16[4096,1024]{1,0:T(8,128)(2,1)} %bitcast.74), kind=kOutput, calls=%fused_computation.22 | convolution fusion | flops 2147745792 | bytes 11010048 | tf_op jit(solution)/shard_map/dot_general | solution.py:124
  501.2 16.5 %while.10 = (s32[]{:T(128)}, f32[1024]{0:T(1024)S(1)}, f32[1024]{0:T(1024)S(1)}, f32[1024]{0:T(1024)S(1)}, s32[]{:T(128)}) while((s32[]{:T(128)}, f32[1024]{0:T(1024)S(1)}, f32[1024]{0:T(1024)S(1)}, f32[1024]{0:T(1024)S(1)}, s32[]{:T(128)}) %tuple.62), condition=%wide.region_6.7_spmd, body=%wide.region_5.6_spmd.sunk | while | flops 2050 | bytes 32869 | solution.py:169
  (275 shorter events, 154.0 us)
Async XLA Ops:
  7.2 394.7 %copy-start = (bf16[4,256,256]{2,1,0:T(8,128)(2,1)S(1)}, bf16[4,256,256]{2,1,0:T(8,128)(2,1)}, u32[]{:S(2)}) copy-start(bf16[4,256,256]{2,1,0:T(8,128)(2,1)} %param.22) | copy-start | bytes 1572868
  7.2 121.4 %copy-start.3 = (bf16[1024,1024]{1,0:T(8,128)(2,1)S(1)}, bf16[1024,1024]{1,0:T(8,128)(2,1)}, u32[]{:S(2)}) copy-start(bf16[1024,1024]{1,0:T(8,128)(2,1)} %param.20) | copy-start | bytes 6291460
  7.2 123.9 %copy-start.26 = (s32[1024]{0:T(1024)S(1)}, s32[1024]{0:T(1024)}, u32[]{:S(2)}) copy-start(s32[1024]{0:T(1024)} %param.17) | copy-start | bytes 12292
  7.2 254.1 %all-gather.3.cloned.1.call-start = ((), (), s32[]{:S(2)}) async-start(), calls=%async_computation.1 | async-start | bytes 10485760 | tf_op jit(solution)/shard_map/all_gather | solution.py:115
  7.9 311.2 %reduce-scatter.2.cloned.1.call-start = ((), (), s32[]{:S(2)}) async-start(), calls=%async_computation.2 | async-start | bytes 2621440 | tf_op jit(solution)/shard_map/reduce_scatter | solution.py:118
  15.4 12.9 %collective-permute-start.1 = (bf16[256,512]{1,0:T(8,128)(2,1)S(1)}, bf16[256,512]{1,0:T(8,128)(2,1)S(1)}, u32[]{:S(2)}, u32[]{:S(2)}) collective-permute-start(bf16[256,512]{1,0:T(8,128)(2,1)S(1)} %all_gather.9), channel_id=1, source_target_pairs={{0,4},{4,8},{8,12},{1,5},{5,9},{9,13},{2,6},{6,10},{10,14},{3,7},{... | collective-permute-start | bytes 786440 | tf_op jit(solution)/shard_map/ppermute | solution.py:39
  28.3 19.7 %collective-permute-start.2 = (bf16[256,512]{1,0:T(8,128)(2,1)S(1)}, bf16[256,512]{1,0:T(8,128)(2,1)S(1)}, u32[]{:S(2)}, u32[]{:S(2)}) collective-permute-start(bf16[256,512]{1,0:T(8,128)(2,1)S(1)} %collective-permute-done.1), channel_id=1, source_target_pairs={{0,4},{4,8},{8,12},{1,5},{5,9},{9,13},{2,6},{6,10},{10,14},{3,7},{... | collective-permute-start | bytes 786440 | tf_op jit(solution)/shard_map/ppermute | solution.py:39
  48.0 23.8 %collective-permute-start.3 = (bf16[256,512]{1,0:T(8,128)(2,1)S(1)}, bf16[256,512]{1,0:T(8,128)(2,1)S(1)}, u32[]{:S(2)}, u32[]{:S(2)}) collective-permute-start(bf16[256,512]{1,0:T(8,128)(2,1)S(1)} %collective-permute-done.2), channel_id=1, source_target_pairs={{0,4},{4,8},{8,12},{1,5},{5,9},{9,13},{2,6},{6,10},{10,14},{3,7},{... | collective-permute-start | bytes 786440 | tf_op jit(solution)/shard_map/ppermute | solution.py:39
  71.8 21.9 %collective-permute-start.4 = (bf16[256,512]{1,0:T(8,128)(2,1)S(1)}, bf16[256,512]{1,0:T(8,128)(2,1)S(1)}, u32[]{:S(2)}, u32[]{:S(2)}) collective-permute-start(bf16[256,512]{1,0:T(8,128)(2,1)S(1)} %collective-permute-done.3), channel_id=1, source_target_pairs={{0,4},{4,8},{8,12},{1,5},{5,9},{9,13},{2,6},{6,10},{10,14},{3,7},{... | collective-permute-start | bytes 786440 | tf_op jit(solution)/shard_map/ppermute | solution.py:39
  93.7 21.0 %collective-permute-start.5 = (bf16[256,512]{1,0:T(8,128)(2,1)S(1)}, bf16[256,512]{1,0:T(8,128)(2,1)S(1)}, u32[]{:S(2)}, u32[]{:S(2)}) collective-permute-start(bf16[256,512]{1,0:T(8,128)(2,1)S(1)} %collective-permute-done.4), channel_id=1, source_target_pairs={{0,4},{4,8},{8,12},{1,5},{5,9},{9,13},{2,6},{6,10},{10,14},{3,7},{... | collective-permute-start | bytes 786440 | tf_op jit(solution)/shard_map/ppermute | solution.py:39
  114.7 127.8 %copy-start.17 = (bf16[256,512]{1,0:T(8,128)(2,1)}, bf16[256,512]{1,0:T(8,128)(2,1)S(1)}, u32[]{:S(2)}) copy-start(bf16[256,512]{1,0:T(8,128)(2,1)S(1)} %collective-permute-done.5) | copy-start | bytes 786436
  114.7 26.1 %collective-permute-start.6 = (bf16[256,512]{1,0:T(8,128)(2,1)S(1)}, bf16[256,512]{1,0:T(8,128)(2,1)S(1)}, u32[]{:S(2)}, u32[]{:S(2)}) collective-permute-start(bf16[256,512]{1,0:T(8,128)(2,1)S(1)} %collective-permute-done.5), channel_id=1, source_target_pairs={{0,4},{4,8},{8,12},{1,5},{5,9},{9,13},{2,6},{6,10},{10,14},{3,7},{... | collective-permute-start | bytes 786440 | tf_op jit(solution)/shard_map/ppermute | solution.py:39
  128.6 139.9 %collective-permute-start.9 = (bf16[1024,1024]{1,0:T(8,128)(2,1)S(1)}, bf16[1024,1024]{1,0:T(8,128)(2,1)}, u32[]{:S(2)}, u32[]{:S(2)}) collective-permute-start(bf16[1024,1024]{1,0:T(8,128)(2,1)S(1)} %copy-done.3), channel_id=1, source_target_pairs={{0,4},{4,8},{8,12},{12,0},{1,5},{5,9},{9,13},{13,1},{2,6},{6,10},{... | collective-permute-start | bytes 6291464 | tf_op jit(solution)/shard_map/ppermute | solution.py:26
  140.8 101.7 %copy-start.19 = (bf16[256,512]{1,0:T(8,128)(2,1)}, bf16[256,512]{1,0:T(8,128)(2,1)S(1)}, u32[]{:S(2)}) copy-start(bf16[256,512]{1,0:T(8,128)(2,1)S(1)} %collective-permute-done.6) | copy-start | bytes 786436
  140.8 97.2 %collective-permute-start.7 = (bf16[256,512]{1,0:T(8,128)(2,1)S(1)}, bf16[256,512]{1,0:T(8,128)(2,1)}, u32[]{:S(2)}, u32[]{:S(2)}) collective-permute-start(bf16[256,512]{1,0:T(8,128)(2,1)S(1)} %collective-permute-done.6), channel_id=1, source_target_pairs={{0,4},{4,8},{8,12},{1,5},{5,9},{9,13},{2,6},{6,10},{10,14},{3,7},{... | collective-permute-start | bytes 786440 | tf_op jit(solution)/shard_map/ppermute | solution.py:39
  151.5 97.3 %copy-start.10 = (bf16[256,512]{1,0:T(8,128)(2,1)S(1)}, bf16[256,512]{1,0:T(8,128)(2,1)}, u32[]{:S(2)}) copy-start(bf16[256,512]{1,0:T(8,128)(2,1)} %copy-done.9) | copy-start | bytes 786436
  238.0 8.7 %collective-permute-start.8 = (bf16[256,512]{1,0:T(8,128)(2,1)}, bf16[256,512]{1,0:T(8,128)(2,1)S(1)}, u32[]{:S(2)}, u32[]{:S(2)}) collective-permute-start(bf16[256,512]{1,0:T(8,128)(2,1)} %collective-permute-done.7), channel_id=1, source_target_pairs={{0,4},{4,8},{8,12},{1,5},{5,9},{9,13},{2,6},{6,10},{10,14},{3,7},{... | collective-permute-start | bytes 786440 | tf_op jit(solution)/shard_map/ppermute | solution.py:39
  268.4 123.7 %all-gather.5.cloned.1.call-start = ((), (), s32[]{:S(2)}) async-start(), calls=%async_computation.3 | async-start | bytes 2621440 | tf_op jit(solution)/shard_map/all_gather | solution.py:122
  268.5 50.7 %collective-permute-start.10 = (bf16[1024,1024]{1,0:T(8,128)(2,1)}, bf16[1024,1024]{1,0:T(8,128)(2,1)}, u32[]{:S(2)}, u32[]{:S(2)}) collective-permute-start(bf16[1024,1024]{1,0:T(8,128)(2,1)} %collective-permute-done.9), channel_id=1, source_target_pairs={{0,4},{4,8},{8,12},{12,0},{1,5},{5,9},{9,13},{13,1},{2,6},{6,10},{... | collective-permute-start | bytes 6291464 | tf_op jit(solution)/shard_map/ppermute | solution.py:26
  319.2 47.5 %collective-permute-start.11 = (bf16[1024,1024]{1,0:T(8,128)(2,1)}, bf16[1024,1024]{1,0:T(8,128)(2,1)}, u32[]{:S(2)}, u32[]{:S(2)}) collective-permute-start(bf16[1024,1024]{1,0:T(8,128)(2,1)} %collective-permute-done.10), channel_id=1, source_target_pairs={{0,4},{4,8},{8,12},{12,0},{1,5},{5,9},{9,13},{13,1},{2,6},{6,10},{... | collective-permute-start | bytes 6291464 | tf_op jit(solution)/shard_map/ppermute | solution.py:26
  398.5 2.6 collective-permute-start.12
  501.2 5.5 %collective-permute-start = (f32[1024]{0:T(1024)S(1)}, f32[1024]{0:T(1024)S(1)}, u32[]{:S(2)}, u32[]{:S(2)}) collective-permute-start(f32[1024]{0:T(1024)S(1)} %multiply_add_fusion.9), channel_id=1, source_target_pairs={{0,4},{4,8},{8,12},{1,5},{5,9},{9,13},{2,6},{6,10},{10,14},{3,7},{... | collective-permute-start | bytes 12296 | tf_op jit(solution)/shard_map/while/body/eval_jaxpr/ppermute | solution.py:39
  506.7 5.5 %collective-permute-start = (f32[1024]{0:T(1024)S(1)}, f32[1024]{0:T(1024)S(1)}, u32[]{:S(2)}, u32[]{:S(2)}) collective-permute-start(f32[1024]{0:T(1024)S(1)} %multiply_add_fusion.9), channel_id=1, source_target_pairs={{0,4},{4,8},{8,12},{1,5},{5,9},{9,13},{2,6},{6,10},{10,14},{3,7},{... | collective-permute-start | bytes 12296 | tf_op jit(solution)/shard_map/while/body/eval_jaxpr/ppermute | solution.py:39
  512.2 5.5 %collective-permute-start = (f32[1024]{0:T(1024)S(1)}, f32[1024]{0:T(1024)S(1)}, u32[]{:S(2)}, u32[]{:S(2)}) collective-permute-start(f32[1024]{0:T(1024)S(1)} %multiply_add_fusion.9), channel_id=1, source_target_pairs={{0,4},{4,8},{8,12},{1,5},{5,9},{9,13},{2,6},{6,10},{10,14},{3,7},{... | collective-permute-start | bytes 12296 | tf_op jit(solution)/shard_map/while/body/eval_jaxpr/ppermute | solution.py:39
  (38 other events, 891.1 us)
Sparse Core Ops, SparseCore 0:
  9.6 229.0 all-gather.2
  268.5 34.7 reduce-scatter.1
  322.4 24.0 all-gather.4
